TPU v7x, 256 devices: a whole 4x4x8 slice. The times are simulated.
256 devices in a mesh: dp: 32 (over z, x), mp: 8 (over y, core).
Axes of the slice: x: 4, y: 4, z: 8, core: 2. Of those that a mesh axis runs over, the one named last changes fastest.
Arguments:
- tokens: bfloat16 [32768, 8192], P('dp', 'mp'), may hold values from -6 to 6
- value_weight: bfloat16 [8192, 1024], P('mp'), may hold values from -0.0625 to 0.0625
- adapter_down_panels: bfloat16 [96, 64, 8192], P('dp', None, 'mp'), may hold values from -0.0625 to 0.0625
- adapter_up_panels: bfloat16 [96, 64, 1024], P('dp', None, 'mp'), may hold values from -0.75 to 0.75
- cotangent: bfloat16 [32768, 1024], P('dp', 'mp'), may hold values from -6 to 6
- block_list_entry: int32 [1024], P('dp'), may hold values from 0 to 31, as said below
- device_tenant_list: int32 [1024], P('dp'), may hold values from 0 to 95, as said below
- tenant_location_map: int32 [96], replicated, may hold values from 0 to 95, as said below
Outputs:
- values: bfloat16 [32768, 1024], P('dp', 'mp')
- token_gradient: bfloat16 [32768, 8192], P('dp', 'mp')
- grad_a: bfloat16 [96, 64, 8192], P('dp', None, 'mp')
- grad_b: bfloat16 [96, 64, 1024], P('dp', None, 'mp')
Inputs may be any that keep to these rules, and one draw needn't show every extreme that they name: `device_tenant_list`: each entry names a tenant; no tenant stands twice in one list. Of one device's 32 entries, at most 2 name tenants whose storage location tenant_location_map[t] lies on one dp index (tenant_location_map[t] // 3), and every device's list has 2 entries on some one dp index. A permutation: tenant t's panels are row tenant_location_map[t] of adapter_down_panels and adapter_up_panels. `block_list_entry`: every entry of a device's tenant list is named by at least one of that device's row blocks.
All inputs are finite; a program needn't handle non-finite values.
Results may differ from a plain program's by a relative error of at most 0.0057.
Values may be sent and summed in bfloat16 or wider, within the bound.
A program may use at most 128 MiB of HBM per device.

v0:
```python
import jax
import jax.numpy as jnp
from jax import lax
from jax.sharding import PartitionSpec as P

MOST = 2


def compare_table(left, right):
    return left[:, None] == right[None, :]


def shards(
    tokens,
    value_weight,
    adapter_down_panels,
    adapter_up_panels,
    cotangent,
    block_list_entry,
    device_tenant_list,
    tenant_location_map,
):
    rows, width_loc = tokens.shape
    stored_panels, adapter_rank_size, ignored_result = adapter_down_panels.shape
    output_location = adapter_up_panels.shape[2]
    blocks = block_list_entry.shape[0]
    block_rows = rows // blocks
    listed = device_tenant_list.shape[0]
    tenants = tenant_location_map.shape[0]
    capacity = lax.axis_size("dp") * MOST
    slot_ids = jnp.arange(listed, dtype=jnp.int32)
    tenant_ids = jnp.arange(tenants, dtype=jnp.int32)
    storage_location = jnp.sum(
        jnp.where(compare_table(device_tenant_list, tenant_ids), tenant_location_map[None, :], 0),
        axis=1,
    )
    holder = storage_location // stored_panels
    local_row = storage_location % stored_panels
    earlier = slot_ids[:, None] > slot_ids[None, :]
    rank_at = jnp.sum(jnp.where(compare_table(holder, holder) & earlier, 1, 0), axis=1).astype(
        jnp.int32
    )
    position = holder * MOST + rank_at
    canonical = jnp.min(
        jnp.where(compare_table(device_tenant_list, device_tenant_list), slot_ids[None, :], listed),
        axis=1,
    )
    block_canon = jnp.sum(
        jnp.where(compare_table(block_list_entry, slot_ids), canonical[None, :], 0), axis=1
    )
    requests = jnp.zeros((capacity,), jnp.int32).at[position].set(local_row + 1)
    incoming = lax.all_to_all(requests, "dp", split_axis=0, concat_axis=0, tiled=True)
    serve_adapters = compare_table(
        incoming, jnp.arange(1, stored_panels + 1, dtype=jnp.int32)
    ).astype(jnp.bfloat16)
    returned_down_panel = jnp.einsum(
        "vj,jiz->viz", serve_adapters, adapter_down_panels, preferred_element_type=jnp.float32
    ).astype(jnp.bfloat16)
    returned_up_panel = jnp.einsum(
        "wu,une->wne", serve_adapters, adapter_up_panels, preferred_element_type=jnp.float32
    ).astype(jnp.bfloat16)
    got_a, got_b = (
        lax.all_to_all(returned_down_panel, "dp", split_axis=0, concat_axis=0, tiled=True),
        lax.all_to_all(returned_up_panel, "dp", split_axis=0, concat_axis=0, tiled=True),
    )
    slot_a = got_a[position]
    slot_b = got_b[position]
    w_cols = value_weight
    base_flipped_weight = lax.psum_scatter(
        lax.dot_general(
            w_cols, tokens, (((0,), (1,)), ((), ())), preferred_element_type=jnp.float32
        ),
        "mp",
        scatter_dimension=0,
        tiled=True,
    )
    token_blocks = tokens.reshape(blocks, block_rows, width_loc)
    cot_blocks = cotangent.reshape(blocks, block_rows, output_location)
    block_down_panel = slot_a[block_list_entry]
    block_up_panel = slot_b[block_list_entry]
    down_part = jnp.einsum(
        "bnd,brd->bnr", token_blocks, block_down_panel, preferred_element_type=jnp.float32
    )
    down_low = lax.psum(down_part, "mp").astype(jnp.bfloat16)
    adapter_output = jnp.einsum(
        "afq,aqy->afy", down_low, block_up_panel, preferred_element_type=jnp.float32
    ).reshape(rows, output_location)
    values = (base_flipped_weight.T + adapter_output).astype(jnp.bfloat16)
    up_part = jnp.einsum(
        "bnc,brc->bnr", cot_blocks, block_up_panel, preferred_element_type=jnp.float32
    )
    up_grad = lax.psum(up_part, "mp").astype(jnp.bfloat16)
    w_cols = value_weight
    base_backward_pass = lax.dot_general(
        lax.all_gather(cotangent, "mp", axis=1, tiled=True),
        w_cols,
        (((1,), (1,)), ((), ())),
        preferred_element_type=jnp.float32,
    )
    adapter_backward_pass = jnp.einsum(
        "swq,sqj->swj", up_grad, block_down_panel, preferred_element_type=jnp.float32
    ).reshape(rows, width_loc)
    token_gradient = (base_backward_pass + adapter_backward_pass).astype(jnp.bfloat16)
    block_grad_a = jnp.einsum(
        "bnr,bnd->brd", up_grad, token_blocks, preferred_element_type=jnp.float32
    )
    block_grad_b = jnp.einsum(
        "bnr,bnc->brc", down_low, cot_blocks, preferred_element_type=jnp.float32
    )
    gather_slots = compare_table(block_canon, slot_ids).astype(jnp.float32)
    share_a = jnp.einsum(
        "bs,brd->srd", gather_slots, block_grad_a, precision=lax.Precision.HIGHEST
    ).astype(jnp.bfloat16)
    share_b = jnp.einsum(
        "bs,brc->src", gather_slots, block_grad_b, precision=lax.Precision.HIGHEST
    ).astype(jnp.bfloat16)
    send_a = (
        jnp.zeros((capacity, adapter_rank_size, width_loc), jnp.bfloat16).at[position].set(share_a)
    )
    send_b = (
        jnp.zeros((capacity, adapter_rank_size, output_location), jnp.bfloat16)
        .at[position]
        .set(share_b)
    )
    back_a, back_b = (
        lax.all_to_all(send_a, "dp", split_axis=0, concat_axis=0, tiled=True),
        lax.all_to_all(send_b, "dp", split_axis=0, concat_axis=0, tiled=True),
    )
    grad_a = jnp.einsum(
        "qk,qrd->krd", serve_adapters, back_a, preferred_element_type=jnp.float32
    ).astype(jnp.bfloat16)
    grad_b = jnp.einsum(
        "qk,qrc->krc", serve_adapters, back_b, preferred_element_type=jnp.float32
    ).astype(jnp.bfloat16)
    return (values, token_gradient, grad_a, grad_b)


def solution(mesh):
    in_specs = (
        P("dp", "mp"),
        P("mp", None),
        P("dp", None, "mp"),
        P("dp", None, "mp"),
        P("dp", "mp"),
        P("dp"),
        P("dp"),
        P(),
    )
    out_specs = (P("dp", "mp"), P("dp", "mp"), P("dp", None, "mp"), P("dp", None, "mp"))
    return jax.shard_map(shards, mesh=mesh, in_specs=in_specs, out_specs=out_specs, check_vma=False)
```

profile of v0, /device:TPU:127, one launch (start us, length us, event | category | flops | bytes accessed | tf_op | source)
XLA Modules:
  0.0 603.8 jit_solution(13908184175450942226)
XLA Ops:
  7.2 1.0 select_reduce_fusion.3
  8.4 0.7 scatter_custom_fusion
  9.1 0.7 all_to_all.18
  9.8 9.6 %all-to-all-start = ((s32[32,2,1]{1,2,0:T(1,128)}), s32[32,2,1]{1,2,0:T(1,128)S(1)}, u32[]{:S(2)}, u32[]{:S(2)}) async-start(s32[32,2,1]{1,2,0:T(1,128)} %bitcast.5), calls=%async_computation.1 | async-start | bytes 32768 | tf_op jit(solution)/shard_map/all_to_all | solution.py:52
  19.5 4.4 all-to-all-done
  23.9 0.5 broadcast.150
  24.4 0.7 reduce.3
  25.2 1.4 convolution_convert_fusion.1
  26.5 1.6 copy.51
  28.2 8.7 %all-to-all-start.2 = ((bf16[64,64,128]{2,1,0:T(8,128)(2,1)}), bf16[64,64,128]{2,1,0:T(8,128)(2,1)}, u32[]{:S(2)}, u32[]{:S(2)}) async-start(bf16[64,64,128]{2,1,0:T(8,128)(2,1)} %copy.51), calls=%async_computation.3 | async-start | bytes 2097152 | tf_op jit(solution)/shard_map/all_to_all | solution.py:64
  36.9 5.7 convolution_convert_fusion
  42.6 11.3 %copy.49 = bf16[64,64,1024]{2,1,0:T(8,128)(2,1)} copy(bf16[64,64,1024]{2,0,1:T(8,128)(2,1)} %convolution_convert_fusion) | data formatting | bytes 16777216 | tf_op jit(solution)/shard_map/convert_element_type | solution.py:58
  53.9 7.4 %all-to-all-done.2 = bf16[64,64,128]{2,1,0:T(8,128)(2,1)} async-done(((bf16[64,64,128]{2,1,0:T(8,128)(2,1)}), bf16[64,64,128]{2,1,0:T(8,128)(2,1)}, u32[]{:S(2)}, u32[]{:S(2)}) %all-to-all-start.2) | async-done | bytes 1048608 | tf_op jit(solution)/shard_map/all_to_all | solution.py:64
  61.3 19.3 %all-to-all-start.1 = ((bf16[64,64,1024]{2,1,0:T(8,128)(2,1)}), bf16[64,64,1024]{2,1,0:T(8,128)(2,1)}, u32[]{:S(2)}, u32[]{:S(2)}) async-start(bf16[64,64,1024]{2,1,0:T(8,128)(2,1)} %copy.49), calls=%async_computation.2 | async-start | bytes 16777216 | tf_op jit(solution)/shard_map/all_to_all | solution.py:63
  81.0 1.9 gather_fusion.2
  82.9 0.6 gather_fusion.3
  83.5 0.4 convolution_bitcast_fusion
  83.9 184.2 %all-to-all-done.1 = bf16[64,64,1024]{2,1,0:T(8,128)(2,1)} async-done(((bf16[64,64,1024]{2,1,0:T(8,128)(2,1)}), bf16[64,64,1024]{2,1,0:T(8,128)(2,1)}, u32[]{:S(2)}, u32[]{:S(2)}) %all-to-all-start.1) | async-done | bytes 8388640 | tf_op jit(solution)/shard_map/all_to_all | solution.py:63
  268.1 6.2 %gather_fusion = bf16[32,64,1024]{2,1,0:T(8,128)(2,1)} fusion(bf16[64,64,1024]{2,1,0:T(8,128)(2,1)} %all-to-all-done.1, s32[1024]{0:T(1024)S(1)} %pad_clamp_fusion.1), kind=kCustom, calls=%fused_computation | custom fusion | bytes 8388736 | tf_op jit(solution)/shard_map/gather | solution.py:66
  274.3 4.9 gather_fusion.1
  279.2 4.2 convolution_bitcast_fusion.1
  283.4 52.8 %all-reduce.2 = (bf16[32,32,64]{2,1,0:T(8,128)(2,1)}, bf16[32,32,64]{2,1,0:T(8,128)(2,1)}) all-reduce(f32[32,32,64]{2,1,0:T(8,128)} %convolution_bitcast_fusion.1, f32[32,32,64]{2,1,0:T(8,128)S(1)} %convolution_bitcast_fusion), channel_id=1, replica_groups=mesh['dp'=32,'mp'=8] {'mp'}, use_global_device_ids=true, to_apply=%region_4.5 | all-reduce | flops 131072 | bytes 786432 | tf_op jit(solution)/shard_map/psum | solution.py:84
  336.3 1.3 fusion.55
  337.6 1.3 convolution_convert_fusion.2
  339.1 1.2 broadcast_in_dim.80
  340.3 4.4 scatter_fusion.1
  344.7 6.9 %all-to-all-start.4 = ((bf16[64,64,128]{2,1,0:T(8,128)(2,1)}), bf16[64,64,128]{2,1,0:T(8,128)(2,1)}, u32[]{:S(2)}, u32[]{:S(2)}) async-start(bf16[64,64,128]{2,1,0:T(8,128)(2,1)} %scatter_fusion.1), calls=%async_computation.5 | async-start | bytes 2097152 | tf_op jit(solution)/shard_map/all_to_all | solution.py:127
  351.6 1.3 fusion.53
  352.8 7.6 %fusion.5 = bf16[32,64,1024]{2,0,1:T(8,128)(2,1)S(1)} fusion(f32[32,64,1024]{2,1,0:T(8,128)S(1)} %fusion.53, s32[32]{0:T(128)S(1)} %select_reduce_fusion), kind=kOutput, calls=%fused_computation.14 | convolution fusion | flops 807404544 | bytes 12583040 | tf_op jit(solution)/shard_map/bs,brd->srd/dot_general | solution.py:111
  360.5 4.2 copy.54
  364.7 4.3 broadcast_in_dim.77
  369.0 11.3 %scatter_fusion = bf16[64,64,1024]{2,1,0:T(8,128)(2,1)} fusion(bf16[64,64,1024]{2,1,0:T(8,128)(2,1)} %broadcast_in_dim.77, s32[32]{0:T(128)S(1)} %fusion.49, bf16[32,64,1024]{2,1,0:T(8,128)(2,1)} %copy.54), kind=kCustom, calls=%fused_computation.5 | custom fusion | bytes 12583040 | tf_op jit(solution)/shard_map/scatter | solution.py:118
  380.4 9.3 %all-to-all-start.3 = ((bf16[64,64,1024]{2,1,0:T(8,128)(2,1)}), bf16[64,64,1024]{2,1,0:T(8,128)(2,1)}, u32[]{:S(2)}, u32[]{:S(2)}) async-start(bf16[64,64,1024]{2,1,0:T(8,128)(2,1)} %scatter_fusion), calls=%async_computation.4 | async-start | bytes 16777216 | tf_op jit(solution)/shard_map/all_to_all | solution.py:126
  389.7 5.9 fusion.52
  395.7 0.2 all-gather.2.cloned.1.call-start
  395.9 0.5 all-gather.2.cloned.1.call-update
  396.6 0.3 fusion.56
  397.1 39.0 %reduce-scatter.2.cloned.1.call-done = f32[128,1024]{1,0:T(8,128)} async-done(((f32[1024,1024]{1,0:T(8,128)}), f32[128,1024]{1,0:T(8,128)}) %reduce-scatter.2.cloned.1.call-update) | async-done | bytes 524304 | tf_op jit(solution)/shard_map/reduce_scatter | solution.py:69
  436.1 1.1 fusion.13
  437.2 0.8 copy.59
  438.0 4.9 fusion.54
  443.0 25.0 %all-gather.2.cloned.1.call-done = bf16[1024,1024]{1,0:T(8,128)(2,1)} async-done(((bf16[1024,128]{1,0:T(8,128)(2,1)}), bf16[1024,1024]{1,0:T(8,128)(2,1)}) %all-gather.2.cloned.1.call-update) | async-done | bytes 2097168 | tf_op jit(solution)/shard_map/all_gather | solution.py:95
  468.0 7.2 %fusion.4 = bf16[1024,1024]{1,0:T(8,128)(2,1)} fusion(f32[32,32,1024]{2,1,0:T(8,128)} %fusion.54, bf16[1024,1024]{1,0:T(8,128)(2,1)} %all-gather.2.cloned.1.call-done, bf16[1024,1024]{1,0:T(8,128)(2,1)} %param.9), kind=kOutput, calls=%fused_computation.13 | convolution fusion | flops 2149580800 | bytes 10485760 | tf_op jit(solution)/shard_map/dot_general | solution.py:94
  475.1 1.9 convolution_convert_fusion.3
  477.0 0.6 copy.61
  477.6 105.8 %all-to-all-done.3 = bf16[64,64,1024]{2,1,0:T(8,128)(2,1)} async-done(((bf16[64,64,1024]{2,1,0:T(8,128)(2,1)}), bf16[64,64,1024]{2,1,0:T(8,128)(2,1)}, u32[]{:S(2)}, u32[]{:S(2)}) %all-to-all-start.3) | async-done | bytes 8388640 | tf_op jit(solution)/shard_map/all_to_all | solution.py:126
  583.4 12.3 %fusion.8 = bf16[3,64,1024]{2,0,1:T(4,128)(2,1)S(1)} fusion(bf16[64,64,1024]{2,1,0:T(8,128)(2,1)} %all-to-all-done.3, s32[64]{0:T(128)S(1)} %eq.42, s32[3]{0:T(128)S(1)} %iota_add_fusion), kind=kOutput, calls=%fused_computation.16 | convolution fusion | flops 25362624 | bytes 8782092 | tf_op jit(solution)/shard_map/qk,qrd->krd/dot_general | solution.py:129
  595.7 0.9 copy.60
  (29 shorter events, 1.4 us)
Async XLA Ops:
  7.2 272.1 %copy-start = (bf16[1024,1024]{1,0:T(8,128)(2,1)S(1)}, bf16[1024,1024]{1,0:T(8,128)(2,1)}, u32[]{:S(2)}) copy-start(bf16[1024,1024]{1,0:T(8,128)(2,1)} %param.8) | copy-start | bytes 6291460
  7.2 29.7 %copy-start.4 = (bf16[3,64,1024]{2,1,0:T(8,128)(2,1)S(1)}, bf16[3,64,1024]{2,1,0:T(8,128)(2,1)}, u32[]{:S(2)}) copy-start(bf16[3,64,1024]{2,1,0:T(8,128)(2,1)} %param.10) | copy-start | bytes 1179652
  9.8 14.0 %all-to-all-start = ((s32[32,2,1]{1,2,0:T(1,128)}), s32[32,2,1]{1,2,0:T(1,128)S(1)}, u32[]{:S(2)}, u32[]{:S(2)}) async-start(s32[32,2,1]{1,2,0:T(1,128)} %bitcast.5), calls=%async_computation.1 | async-start | bytes 32768 | tf_op jit(solution)/shard_map/all_to_all | solution.py:52
  28.2 33.1 %all-to-all-start.2 = ((bf16[64,64,128]{2,1,0:T(8,128)(2,1)}), bf16[64,64,128]{2,1,0:T(8,128)(2,1)}, u32[]{:S(2)}, u32[]{:S(2)}) async-start(bf16[64,64,128]{2,1,0:T(8,128)(2,1)} %copy.51), calls=%async_computation.3 | async-start | bytes 2097152 | tf_op jit(solution)/shard_map/all_to_all | solution.py:64
  53.9 26.7 %copy-start.6 = (s32[32]{0:T(128)S(1)}, s32[32]{0:T(128)}, u32[]{:S(2)}) copy-start(s32[32]{0:T(128)} %param.13) | copy-start | bytes 388
  53.9 26.7 %copy-start.5 = (s32[32]{0:T(128)S(1)}, s32[32]{0:T(128)}, u32[]{:S(2)}) copy-start(s32[32]{0:T(128)} %param.14) | copy-start | bytes 388
  53.9 29.7 %copy-start.1 = (bf16[1024,128]{1,0:T(8,128)(2,1)S(1)}, bf16[1024,128]{1,0:T(8,128)(2,1)}, u32[]{:S(2)}) copy-start(bf16[1024,128]{1,0:T(8,128)(2,1)} %param.12) | copy-start | bytes 786436
  61.3 206.8 %all-to-all-start.1 = ((bf16[64,64,1024]{2,1,0:T(8,128)(2,1)}), bf16[64,64,1024]{2,1,0:T(8,128)(2,1)}, u32[]{:S(2)}, u32[]{:S(2)}) async-start(bf16[64,64,1024]{2,1,0:T(8,128)(2,1)} %copy.49), calls=%async_computation.2 | async-start | bytes 16777216 | tf_op jit(solution)/shard_map/all_to_all | solution.py:63
  336.3 15.3 %copy-start.3 = (bf16[32,32,64]{2,1,0:T(8,128)(2,1)S(1)}, bf16[32,32,64]{2,1,0:T(8,128)(2,1)}, u32[]{:S(2)}) copy-start(bf16[32,32,64]{2,1,0:T(8,128)(2,1)} %get-tuple-element.21) | copy-start | bytes 393220
  344.7 35.7 %all-to-all-start.4 = ((bf16[64,64,128]{2,1,0:T(8,128)(2,1)}), bf16[64,64,128]{2,1,0:T(8,128)(2,1)}, u32[]{:S(2)}, u32[]{:S(2)}) async-start(bf16[64,64,128]{2,1,0:T(8,128)(2,1)} %scatter_fusion.1), calls=%async_computation.5 | async-start | bytes 2097152 | tf_op jit(solution)/shard_map/all_to_all | solution.py:127
  380.4 203.1 %all-to-all-start.3 = ((bf16[64,64,1024]{2,1,0:T(8,128)(2,1)}), bf16[64,64,1024]{2,1,0:T(8,128)(2,1)}, u32[]{:S(2)}, u32[]{:S(2)}) async-start(bf16[64,64,1024]{2,1,0:T(8,128)(2,1)} %scatter_fusion), calls=%async_computation.4 | async-start | bytes 16777216 | tf_op jit(solution)/shard_map/all_to_all | solution.py:126
  389.6 46.4 %reduce-scatter.2.cloned.1.call-start = ((), (), s32[]{:S(2)}) async-start(), calls=%async_computation.6 | async-start | bytes 4718592 | tf_op jit(solution)/shard_map/reduce_scatter | solution.py:69
  395.6 0.9 copy-start.2
  395.7 72.3 %all-gather.2.cloned.1.call-start = ((), (), s32[]{:S(2)}) async-start(), calls=%async_computation.7 | async-start | bytes 2359296 | tf_op jit(solution)/shard_map/all_gather | solution.py:95
Sparse Core Ops, SparseCore 0:
  395.8 40.2 reduce-scatter.1
  437.9 30.0 all-gather.1
where the time goes:
time: 613 us; the launch traced here: 604 us
  waiting for transfers between devices  366 us (60%)
  local copies, waits for them, and re-layouts  57 us (9%)
  matrix products  55.7 us (9%)
  starting transfers between devices  54 us (9%)
  blocking collectives  52.8 us (9%)
  between operations  14.7 us (2%)
    all_to_all x1, waiting for transfers between devices, shards(): lax.all_to_all(returned_down_panel, 'dp', split_axis=0, concat_axis=0, ti...  184 us
    all_to_all x1, waiting for transfers between devices, shards(): lax.all_to_all(send_a, 'dp', split_axis=0, concat_axis=0, tiled=True)  106 us
    psum x1, blocking collectives, shards(): down_low = lax.psum(down_part, 'mp').astype(jnp.bfloat16)  52.8 us
    reduce_scatter x1, waiting for transfers between devices, shards(): lax.psum_scatter(lax.dot_general(w_cols, tokens, (((0,), (1,)), ((), ()))...  39 us
    all_gather x1, waiting for transfers between devices, shards(): lax.all_gather(cotangent, 'mp', axis=1, tiled=True)  25 us
    all_to_all x1, starting transfers between devices, shards(): lax.all_to_all(returned_down_panel, 'dp', split_axis=0, concat_axis=0, ti...  19.3 us
    dot_general x1, matrix products, shards(): jnp.einsum('qk,qrd->krd', serve_adapters, back_a, preferred_element_type=...  12.3 us
  transfers between devices with their start and end apart: 7, of which 6 were waited for; matrix products, arithmetic and copies ran while one was open for 12% of the time, Pallas kernels for 0%

commit v1 on v0

--- a/solution.py
+++ b/solution.py
@@ -1,9 +1,17 @@
+import functools
 import jax
 import jax.numpy as jnp
 from jax import lax
 from jax.sharding import PartitionSpec as P
 
 MOST = 2
+
+
+def order_scales(here_x, peer_axis):
+    return jnp.sum(jax.lax.all_gather(here_x, peer_axis), 0)
+
+
+boxes_report = functools.partial(order_scales, peer_axis="mp")
 
 
 def compare_table(left, right):
@@ -81,7 +89,7 @@
     down_part = jnp.einsum(
         "bnd,brd->bnr", token_blocks, block_down_panel, preferred_element_type=jnp.float32
     )
-    down_low = lax.psum(down_part, "mp").astype(jnp.bfloat16)
+    down_low = boxes_report(down_part).astype(jnp.bfloat16)
     adapter_output = jnp.einsum(
         "afq,aqy->afy", down_low, block_up_panel, preferred_element_type=jnp.float32
     ).reshape(rows, output_location)

time: 613 us -> 509 us (0.83)
  the two profiles are of different devices: /device:TPU:127 before, /device:TPU:18 now
where the time goes in v1:
time: 509 us; the launch traced here: 500 us
  waiting for transfers between devices  282 us (55%)
  local copies, waits for them, and re-layouts  60.1 us (12%)
  matrix products  55.3 us (11%)
  starting transfers between devices  43.9 us (9%)
  blocking collectives  38 us (7%)
  between operations  14.4 us (3%)
  other arithmetic  6.19 us (1%)
    all_to_all x1, waiting for transfers between devices, shards(): lax.all_to_all(send_a, 'dp', split_axis=0, concat_axis=0, tiled=True)  126 us
    all_to_all x1, waiting for transfers between devices, shards(): lax.all_to_all(returned_down_panel, 'dp', split_axis=0, concat_axis=0, ti...  109 us
    psum x1, blocking collectives, shards(): up_grad = lax.psum(up_part, 'mp').astype(jnp.bfloat16)  38 us
    all_gather x1, waiting for transfers between devices, order_scales(): return jnp.sum(jax.lax.all_gather(here_x, peer_axis), 0)  27.7 us
    all_to_all x1, starting transfers between devices, shards(): lax.all_to_all(send_a, 'dp', split_axis=0, concat_axis=0, tiled=True)  12.6 us
    dot_general x1, matrix products, shards(): jnp.einsum('qk,qrd->krd', serve_adapters, back_a, preferred_element_type=...  12.3 us
    all_to_all x1, starting transfers between devices, shards(): lax.all_to_all(requests, 'dp', split_axis=0, concat_axis=0, tiled=True)  11.6 us
    scatter x1, local copies, waits for them, and re-layouts, shards(): jnp.zeros((capacity, adapter_rank_size, width_loc), jnp.bfloat16)  11.3 us
  transfers between devices with their start and end apart: 8, of which 5 were waited for; matrix products, arithmetic and copies ran while one was open for 22% of the time, Pallas kernels for 0%

profile of v1, /device:TPU:18, one launch (start us, length us, event | category | flops | bytes accessed | tf_op | source)
XLA Modules:
  0.0 499.8 jit_solution(2229507911706907366)
XLA Ops:
  7.2 1.0 select_reduce_fusion.3
  8.4 0.7 scatter_custom_fusion
  9.1 0.7 all_to_all.18
  9.8 11.6 %all-to-all-start = ((s32[32,2,1]{1,2,0:T(1,128)}), s32[32,2,1]{1,2,0:T(1,128)S(1)}, u32[]{:S(2)}, u32[]{:S(2)}) async-start(s32[32,2,1]{1,2,0:T(1,128)} %bitcast.5), calls=%async_computation.1 | async-start | bytes 32768 | tf_op jit(solution)/shard_map/all_to_all | solution.py:60
  21.5 8.4 %all-to-all-done = s32[32,2,1]{1,2,0:T(1,128)S(1)} async-done(((s32[32,2,1]{1,2,0:T(1,128)}), s32[32,2,1]{1,2,0:T(1,128)S(1)}, u32[]{:S(2)}, u32[]{:S(2)}) %all-to-all-start) | async-done | bytes 288 | tf_op jit(solution)/shard_map/all_to_all | solution.py:60
  29.9 0.5 broadcast.150
  30.4 0.7 reduce.3
  31.2 1.4 convolution_convert_fusion.1
  32.6 1.6 copy.51
  34.2 5.7 %all-to-all-start.2 = ((bf16[64,64,128]{2,1,0:T(8,128)(2,1)}), bf16[64,64,128]{2,1,0:T(8,128)(2,1)}, u32[]{:S(2)}, u32[]{:S(2)}) async-start(bf16[64,64,128]{2,1,0:T(8,128)(2,1)} %copy.51), calls=%async_computation.3 | async-start | bytes 2097152 | tf_op jit(solution)/shard_map/all_to_all | solution.py:72
  39.9 5.7 %convolution_convert_fusion = bf16[64,64,1024]{2,0,1:T(8,128)(2,1)} fusion(bf16[3,64,1024]{2,1,0:T(8,128)(2,1)S(1)} %copy-done.3, s32[64]{0:T(128)S(1)} %eq.42, s32[3]{0:T(128)S(1)} %iota_add_fusion), kind=kOutput, calls=%fused_computation.11 | convolution fusion | flops 29360320 | bytes 8782092 | tf_op jit(solution)/shard_map/vj,jiz->viz/dot_general | solution.py:64
  45.6 11.3 %copy.49 = bf16[64,64,1024]{2,1,0:T(8,128)(2,1)} copy(bf16[64,64,1024]{2,0,1:T(8,128)(2,1)} %convolution_convert_fusion) | data formatting | bytes 16777216 | tf_op jit(solution)/shard_map/convert_element_type | solution.py:66
  56.9 10.1 %all-to-all-done.2 = bf16[64,64,128]{2,1,0:T(8,128)(2,1)} async-done(((bf16[64,64,128]{2,1,0:T(8,128)(2,1)}), bf16[64,64,128]{2,1,0:T(8,128)(2,1)}, u32[]{:S(2)}, u32[]{:S(2)}) %all-to-all-start.2) | async-done | bytes 1048608 | tf_op jit(solution)/shard_map/all_to_all | solution.py:72
  67.0 5.6 %all-to-all-start.1 = ((bf16[64,64,1024]{2,1,0:T(8,128)(2,1)}), bf16[64,64,1024]{2,1,0:T(8,128)(2,1)}, u32[]{:S(2)}, u32[]{:S(2)}) async-start(bf16[64,64,1024]{2,1,0:T(8,128)(2,1)} %copy.49), calls=%async_computation.2 | async-start | bytes 16777216 | tf_op jit(solution)/shard_map/all_to_all | solution.py:71
  73.0 2.6 gather_fusion.2
  75.7 1.7 gather_fusion.3
  77.4 1.2 convolution_bitcast_fusion
  78.5 38.0 %all-reduce.1 = bf16[32,32,64]{2,1,0:T(8,128)(2,1)S(1)} all-reduce(f32[32,32,64]{2,1,0:T(8,128)} %convolution_bitcast_fusion), channel_id=1, replica_groups=mesh['dp'=32,'mp'=8] {'mp'}, use_global_device_ids=true, to_apply=%region_5.6 | all-reduce | flops 65536 | bytes 393216 | tf_op jit(solution)/shard_map/psum | solution.py:100
  116.6 1.3 fusion.53
  117.9 7.6 %fusion.5 = bf16[32,64,1024]{2,0,1:T(8,128)(2,1)S(1)} fusion(f32[32,64,1024]{2,1,0:T(8,128)S(1)} %fusion.53, s32[32]{0:T(128)S(1)} %select_reduce_fusion), kind=kOutput, calls=%fused_computation.14 | convolution fusion | flops 807404544 | bytes 12583040 | tf_op jit(solution)/shard_map/bs,brd->srd/dot_general | solution.py:119
  125.5 4.3 copy.54
  129.8 4.3 broadcast_in_dim.77
  134.1 11.3 %scatter_fusion = bf16[64,64,1024]{2,1,0:T(8,128)(2,1)} fusion(bf16[64,64,1024]{2,1,0:T(8,128)(2,1)} %broadcast_in_dim.77, s32[32]{0:T(128)S(1)} %fusion.49, bf16[32,64,1024]{2,1,0:T(8,128)(2,1)} %copy.54), kind=kCustom, calls=%fused_computation.5 | custom fusion | bytes 12583040 | tf_op jit(solution)/shard_map/scatter | solution.py:126
  145.5 108.6 %all-to-all-done.1 = bf16[64,64,1024]{2,1,0:T(8,128)(2,1)} async-done(((bf16[64,64,1024]{2,1,0:T(8,128)(2,1)}), bf16[64,64,1024]{2,1,0:T(8,128)(2,1)}, u32[]{:S(2)}, u32[]{:S(2)}) %all-to-all-start.1) | async-done | bytes 8388640 | tf_op jit(solution)/shard_map/all_to_all | solution.py:71
  254.1 12.6 %all-to-all-start.3 = ((bf16[64,64,1024]{2,1,0:T(8,128)(2,1)}), bf16[64,64,1024]{2,1,0:T(8,128)(2,1)}, u32[]{:S(2)}, u32[]{:S(2)}) async-start(bf16[64,64,1024]{2,1,0:T(8,128)(2,1)} %scatter_fusion), calls=%async_computation.4 | async-start | bytes 16777216 | tf_op jit(solution)/shard_map/all_to_all | solution.py:134
  266.8 6.2 %gather_fusion = bf16[32,64,1024]{2,1,0:T(8,128)(2,1)} fusion(bf16[64,64,1024]{2,1,0:T(8,128)(2,1)} %all-to-all-done.1, s32[1024]{0:T(1024)S(1)} %pad_clamp_fusion.1), kind=kCustom, calls=%fused_computation | custom fusion | bytes 8388736 | tf_op jit(solution)/shard_map/gather | solution.py:74
  273.0 5.0 gather_fusion.1
  277.9 4.2 convolution_bitcast_fusion.1
  282.2 0.7 all-gather.4.cloned.1.call-update
  283.0 5.9 %fusion.52 = f32[1024,1024]{1,0:T(8,128)} fusion(bf16[1024,1024]{1,0:T(8,128)(2,1)} %param.9, bf16[1024,1024]{1,0:T(8,128)(2,1)S(1)} %copy-done), kind=kOutput, calls=%fused_computation.79 | convolution fusion | flops 2147483648 | bytes 8388608 | tf_op jit(solution)/shard_map/dot_general | solution.py:78
  288.9 27.7 %all-gather.6.cloned.1.call-done = f32[256,32,64]{2,1,0:T(8,128)} async-done(((f32[32,32,64]{2,1,0:T(8,128)}), f32[256,32,64]{2,1,0:T(8,128)}) %all-gather.6.cloned.1.call-update) | async-done | bytes 2097168 | tf_op jit(solution)/shard_map/all_gather | solution.py:11
  316.6 2.8 reduce_sum.41
  319.4 0.3 fusion.55
  319.8 1.3 convolution_convert_fusion.2
  321.1 1.0 copy.57
  322.1 1.3 broadcast_in_dim.80
  323.4 4.8 scatter_fusion.1
  328.2 126.4 %all-to-all-done.3 = bf16[64,64,1024]{2,1,0:T(8,128)(2,1)} async-done(((bf16[64,64,1024]{2,1,0:T(8,128)(2,1)}), bf16[64,64,1024]{2,1,0:T(8,128)(2,1)}, u32[]{:S(2)}, u32[]{:S(2)}) %all-to-all-start.3) | async-done | bytes 8388640 | tf_op jit(solution)/shard_map/all_to_all | solution.py:134
  454.5 8.2 %all-to-all-start.4 = ((bf16[64,64,128]{2,1,0:T(8,128)(2,1)}), bf16[64,64,128]{2,1,0:T(8,128)(2,1)}, u32[]{:S(2)}, u32[]{:S(2)}) async-start(bf16[64,64,128]{2,1,0:T(8,128)(2,1)} %scatter_fusion.1), calls=%async_computation.5 | async-start | bytes 2097152 | tf_op jit(solution)/shard_map/all_to_all | solution.py:135
  462.7 4.8 fusion.54
  467.5 7.2 %fusion.4 = bf16[1024,1024]{1,0:T(8,128)(2,1)} fusion(f32[32,32,1024]{2,1,0:T(8,128)} %fusion.54, bf16[1024,1024]{1,0:T(8,128)(2,1)} %all-gather.4.cloned.1.call-done, bf16[1024,1024]{1,0:T(8,128)(2,1)} %param.9), kind=kOutput, calls=%fused_computation.13 | convolution fusion | flops 2149580800 | bytes 10485760 | tf_op jit(solution)/shard_map/dot_general | solution.py:102
  474.7 12.3 %fusion.8 = bf16[3,64,1024]{2,0,1:T(4,128)(2,1)S(1)} fusion(bf16[64,64,1024]{2,1,0:T(8,128)(2,1)} %all-to-all-done.3, s32[64]{0:T(128)S(1)} %eq.42, s32[3]{0:T(128)S(1)} %iota_add_fusion), kind=kOutput, calls=%fused_computation.16 | convolution fusion | flops 25362624 | bytes 8782092 | tf_op jit(solution)/shard_map/qk,qrd->krd/dot_general | solution.py:137
  487.0 0.9 copy.60
  487.9 0.3 fusion.56
  488.4 1.1 fusion.13
  489.5 0.8 copy.59
  490.3 1.9 convolution_convert_fusion.3
  492.2 0.6 copy.61
  (31 shorter events, 1.1 us)
Async XLA Ops:
  7.2 109.4 %copy-start = (bf16[1024,1024]{1,0:T(8,128)(2,1)S(1)}, bf16[1024,1024]{1,0:T(8,128)(2,1)}, u32[]{:S(2)}) copy-start(bf16[1024,1024]{1,0:T(8,128)(2,1)} %param.8) | copy-start | bytes 6291460
  7.2 32.7 %copy-start.3 = (bf16[3,64,1024]{2,1,0:T(8,128)(2,1)S(1)}, bf16[3,64,1024]{2,1,0:T(8,128)(2,1)}, u32[]{:S(2)}) copy-start(bf16[3,64,1024]{2,1,0:T(8,128)(2,1)} %param.10) | copy-start | bytes 1179652
  9.8 20.1 %all-to-all-start = ((s32[32,2,1]{1,2,0:T(1,128)}), s32[32,2,1]{1,2,0:T(1,128)S(1)}, u32[]{:S(2)}, u32[]{:S(2)}) async-start(s32[32,2,1]{1,2,0:T(1,128)} %bitcast.5), calls=%async_computation.1 | async-start | bytes 32768 | tf_op jit(solution)/shard_map/all_to_all | solution.py:60
  34.2 32.7 %all-to-all-start.2 = ((bf16[64,64,128]{2,1,0:T(8,128)(2,1)}), bf16[64,64,128]{2,1,0:T(8,128)(2,1)}, u32[]{:S(2)}, u32[]{:S(2)}) async-start(bf16[64,64,128]{2,1,0:T(8,128)(2,1)} %copy.51), calls=%async_computation.3 | async-start | bytes 2097152 | tf_op jit(solution)/shard_map/all_to_all | solution.py:72
  56.9 15.7 %copy-start.5 = (s32[32]{0:T(128)S(1)}, s32[32]{0:T(128)}, u32[]{:S(2)}) copy-start(s32[32]{0:T(128)} %param.13) | copy-start | bytes 388
  56.9 15.7 %copy-start.4 = (s32[32]{0:T(128)S(1)}, s32[32]{0:T(128)}, u32[]{:S(2)}) copy-start(s32[32]{0:T(128)} %param.14) | copy-start | bytes 388
  56.9 20.4 %copy-start.1 = (bf16[1024,128]{1,0:T(8,128)(2,1)S(1)}, bf16[1024,128]{1,0:T(8,128)(2,1)}, u32[]{:S(2)}) copy-start(bf16[1024,128]{1,0:T(8,128)(2,1)} %param.12) | copy-start | bytes 786436
  67.0 187.1 %all-to-all-start.1 = ((bf16[64,64,1024]{2,1,0:T(8,128)(2,1)}), bf16[64,64,1024]{2,1,0:T(8,128)(2,1)}, u32[]{:S(2)}, u32[]{:S(2)}) async-start(bf16[64,64,1024]{2,1,0:T(8,128)(2,1)} %copy.49), calls=%async_computation.2 | async-start | bytes 16777216 | tf_op jit(solution)/shard_map/all_to_all | solution.py:71
  254.1 200.4 %all-to-all-start.3 = ((bf16[64,64,1024]{2,1,0:T(8,128)(2,1)}), bf16[64,64,1024]{2,1,0:T(8,128)(2,1)}, u32[]{:S(2)}, u32[]{:S(2)}) async-start(bf16[64,64,1024]{2,1,0:T(8,128)(2,1)} %scatter_fusion), calls=%async_computation.4 | async-start | bytes 16777216 | tf_op jit(solution)/shard_map/all_to_all | solution.py:134
  266.7 49.9 %all-gather.6.cloned.1.call-start = ((), (), s32[]{:S(2)}) async-start(), calls=%async_computation.8 | async-start | bytes 4718592 | tf_op jit(solution)/shard_map/all_gather | solution.py:11
  282.2 185.4 %all-gather.4.cloned.1.call-start = ((), (), s32[]{:S(2)}) async-start(), calls=%async_computation.7 | async-start | bytes 2359296 | tf_op jit(solution)/shard_map/all_gather | solution.py:103
  282.9 205.5 %reduce-scatter.2.cloned.1.call-start = ((), (), s32[]{:S(2)}) async-start(), calls=%async_computation.6 | async-start | bytes 4718592 | tf_op jit(solution)/shard_map/reduce_scatter | solution.py:77
  288.9 30.5 %copy-start.2 = (bf16[1024,128]{1,0:T(8,128)(2,1)S(1)}, bf16[1024,128]{1,0:T(8,128)(2,1)}, u32[]{:S(2)}) copy-start(bf16[1024,128]{1,0:T(8,128)(2,1)} %param.12) | copy-start | bytes 786436
  454.5 35.8 %all-to-all-start.4 = ((bf16[64,64,128]{2,1,0:T(8,128)(2,1)}), bf16[64,64,128]{2,1,0:T(8,128)(2,1)}, u32[]{:S(2)}, u32[]{:S(2)}) async-start(bf16[64,64,128]{2,1,0:T(8,128)(2,1)} %scatter_fusion.1), calls=%async_computation.5 | async-start | bytes 2097152 | tf_op jit(solution)/shard_map/all_to_all | solution.py:135
Sparse Core Ops, SparseCore 0:
  282.3 34.2 all-gather.5
  318.4 30.8 all-gather.3
  351.8 37.1 reduce-scatter.1
